TPU v7x, 256 devices: a whole 4x4x8 slice. The times are simulated.
256 devices in a mesh: tp: 32 (over z, x_lo, core), dp: 8 (over x_hi, y).
Axes of the slice: x: 4 (x_hi: 2, x_lo: 2; x = x_hi * 2 + x_lo), y: 4, z: 8, core: 2. Of those that a mesh axis runs over, the one named last changes fastest.
Arguments:
- forget_inputs: bfloat16 [4096, 8192], P(('tp', 'dp')), may hold values from -6 to 6
- gate_pre: bfloat16 [4096, 16384], P('dp', 'tp'), may hold values from -6 to 6
- up_pre: bfloat16 [4096, 16384], P('dp', 'tp'), may hold values from -6 to 6
- hidden_grad: bfloat16 [4096, 16384], P('dp', 'tp'), may hold values from -6 to 6
- gate_weight: bfloat16 [8192, 16384], P('dp', 'tp'), may hold values from -0.0625 to 0.0625
- up_weight: bfloat16 [8192, 16384], P('dp', 'tp'), may hold values from -0.0625 to 0.0625
- retain_gate: float32 [8192, 16384], P('dp', 'tp'), may hold values from 0.002 to 0.2
- retain_up: float32 [8192, 16384], P('dp', 'tp'), may hold values from 0.002 to 0.2
Outputs:
- new_gate: bfloat16 [8192, 16384], P('dp', 'tp')
- new_up: bfloat16 [8192, 16384], P('dp', 'tp')
All inputs are finite; a program needn't handle non-finite values.
Results may differ from a plain program's by a relative error of at most 0.0064.
Values may be sent and summed in bfloat16 or wider, within the bound.
No kernel may reach another device: no remote copies, remote signals or barrier semaphores. Data moves between devices by JAX's collectives and lax.ppermute only.
A program may use at most 128 MiB of HBM per device.

v0:
```python
import jax
import jax.numpy as jnp
from jax import lax
from jax.sharding import PartitionSpec as P

select_ratio = 10.0
dampen_ratio = 10.0


def accumulate(piece, deltas):
    return lax.dot_general(
        piece, deltas, (((0,), (0,)), ((), ())), preferred_element_type=jnp.float32
    )


def dampened(weight, retain, summed, count):
    forget = summed * summed / count
    factor = dampen_ratio * retain / jnp.maximum(forget, select_ratio * retain)
    return (weight.astype(jnp.float32) * factor).astype(jnp.bfloat16)


def body(
    forget_inputs, gate_pre, up_pre, hidden_grad, gate_weight, up_weight, retain_gate, retain_up
):
    gate_val = gate_pre.astype(jnp.float32)
    up_val = up_pre.astype(jnp.float32)
    grad_val = hidden_grad.astype(jnp.float32)
    sig = jax.nn.sigmoid(gate_val)
    gate_delta = (grad_val * up_val * sig * (1.0 + gate_val * (1.0 - sig))).astype(jnp.bfloat16)
    up_delta = (grad_val * gate_val * sig).astype(jnp.bfloat16)
    gate_all, up_all = (
        lax.all_gather(gate_delta, "dp", axis=0, tiled=True),
        lax.all_gather(up_delta, "dp", axis=0, tiled=True),
    )
    columns = lax.all_to_all(forget_inputs, "dp", split_axis=1, concat_axis=0, tiled=True)
    count = float(gate_all.shape[0])
    gate_sum = accumulate(lax.all_gather(columns, "tp", axis=0, tiled=True), gate_all)
    up_sum = accumulate(lax.all_gather(columns, "tp", axis=0, tiled=True), up_all)
    new_gate = dampened(gate_weight, retain_gate, gate_sum, count)
    new_up = dampened(up_weight, retain_up, up_sum, count)
    return (new_gate, new_up)


def solution(mesh):
    placed = (
        P(("tp", "dp"), None),
        P("dp", "tp"),
        P("dp", "tp"),
        P("dp", "tp"),
        P("dp", "tp"),
        P("dp", "tp"),
        P("dp", "tp"),
        P("dp", "tp"),
    )
    return jax.shard_map(
        body, mesh=mesh, in_specs=placed, out_specs=(P("dp", "tp"), P("dp", "tp")), check_vma=False
    )
```

profile of v0, /device:TPU:1, one launch (start us, length us, event | category | flops | bytes accessed | tf_op | source)
XLA Modules:
  0.0 259.4 jit_solution(13563033080113747796)
XLA Ops:
  7.2 0.0 copy-start.7
  7.2 0.0 copy-start
  7.2 0.0 all-gather.4.cloned.1.call-start
  7.2 3.0 %fusion.12 = (bf16[512,512]{1,0:T(8,128)(2,1)}, bf16[512,512]{1,0:T(8,128)(2,1)}) fusion(bf16[512,512]{1,0:T(8,128)(2,1)} %param.9, bf16[512,512]{1,0:T(8,128)(2,1)} %param.11, bf16[512,512]{1,0:T(8,128)(2,1)} %param.10), kind=kLoop, calls=%fused_computation.18 | loop fusion | flops 4194304 | bytes 2621440 | tf_op jit(solution)/shard_map/convert_element_type | solution.py:30
  10.2 0.0 all-gather.4.cloned.1.call-update
  10.3 0.0 all-gather.6.cloned.1.call-start
  10.3 0.0 copy-done.7
  10.4 15.0 %all_to_all.19 = bf16[16,8,1024]{2,0,1:T(8,128)(2,1)} all-to-all(bf16[16,8,1024]{2,0,1:T(8,128)(2,1)S(1)} %bitcast.16), channel_id=1, replica_groups=mesh['tp'=32,'dp'=8] {'dp'}, dimensions={1} | all-to-all | bytes 524288 | tf_op jit(solution)/shard_map/all_to_all | solution.py:35
  25.3 0.0 all-gather.6.cloned.1.call-update
  25.3 0.0 all-gather.8.cloned.1.call-start
  25.4 0.7 all-gather.8.cloned.1.call-update
  26.1 0.0 copy-done
  26.1 0.0 copy-start.4
  26.1 1.9 copy.30
  28.0 0.0 copy-done.4
  28.0 0.0 copy-start.1
  28.0 1.3 copy.29
  29.3 0.7 copy-done.1
  30.0 0.0 copy-start.5
  30.0 1.8 copy.33
  31.8 0.0 copy-done.5
  31.8 0.0 copy-start.3
  31.9 1.3 copy.32
  33.2 57.3 %all-gather.4.cloned.1.call-done = bf16[4096,512]{1,0:T(8,128)(2,1)} async-done(((bf16[512,512]{1,0:T(8,128)(2,1)}), bf16[4096,512]{1,0:T(8,128)(2,1)}) %all-gather.4.cloned.1.call-update) | async-done | bytes 4194320 | tf_op jit(solution)/shard_map/all_gather | solution.py:32
  90.4 72.6 %all-gather.6.cloned.1.call-done = bf16[4096,1024]{1,0:T(8,128)(2,1)} async-done(((bf16[128,1024]{1,0:T(8,128)(2,1)}), bf16[4096,1024]{1,0:T(8,128)(2,1)}) %all-gather.6.cloned.1.call-update) | async-done | bytes 8388624 | tf_op jit(solution)/shard_map/all_gather | solution.py:37
  163.1 0.0 copy-done.3
  163.1 0.0 copy-start.6
  163.1 10.7 %fusion.1 = bf16[1024,512]{0,1:T(8,128)(2,1)} fusion(f32[1024,512]{0,1:T(8,128)S(1)} %copy-done.3, bf16[1024,512]{0,1:T(8,128)(2,1)} %copy.29, bf16[4096,512]{1,0:T(8,128)(2,1)} %all-gather.4.cloned.1.call-done, bf16[4096,1024]{1,0:T(8,128)(2,1)} %all-gather.6.cloned.1.call-done), kind=kOutput, calls=%fused_computation.3 | convolution fusion | flops 4299161600 | bytes 16777216 | tf_op jit(solution)/shard_map/dot_general | solution.py:11
  173.8 0.0 copy-start.2
  173.8 2.4 copy.34
  176.2 63.8 %all-gather.8.cloned.1.call-done = bf16[4096,512]{1,0:T(8,128)(2,1)} async-done(((bf16[512,512]{1,0:T(8,128)(2,1)}), bf16[4096,512]{1,0:T(8,128)(2,1)}) %all-gather.8.cloned.1.call-update) | async-done | bytes 4194320 | tf_op jit(solution)/shard_map/all_gather | solution.py:33
  240.0 0.0 copy-done.6
  240.0 0.0 copy-done.2
  240.0 10.6 %fusion.3 = bf16[1024,512]{0,1:T(8,128)(2,1)} fusion(f32[1024,512]{0,1:T(8,128)S(1)} %copy-done.2, bf16[1024,512]{0,1:T(8,128)(2,1)S(1)} %copy-done.6, bf16[4096,512]{1,0:T(8,128)(2,1)} %all-gather.8.cloned.1.call-done, bf16[4096,1024]{1,0:T(8,128)(2,1)} %all-gather.6.cloned.1.call-done), kind=kOutput, calls=%fused_computation.5 | convolution fusion | flops 4299161600 | bytes 16777216 | tf_op jit(solution)/shard_map/dot_general | solution.py:11
  250.6 2.3 copy.35
  (1 shorter events, 0.0 us)
Async XLA Ops:
  7.2 3.2 %copy-start.7 = (bf16[16,8192]{1,0:T(8,128)(2,1)S(1)}, bf16[16,8192]{1,0:T(8,128)(2,1)}, u32[]{:S(2)}) copy-start(bf16[16,8192]{1,0:T(8,128)(2,1)} %param.8) | copy-start | bytes 786436
  7.2 18.9 %copy-start = (f32[1024,512]{1,0:T(8,128)S(1)}, f32[1024,512]{1,0:T(8,128)}, u32[]{:S(2)}) copy-start(f32[1024,512]{1,0:T(8,128)} %param.14) | copy-start | bytes 6291460
  7.2 83.2 %all-gather.4.cloned.1.call-start = ((), (), s32[]{:S(2)}) async-start(), calls=%async_computation.1 | async-start | bytes 4718592 | tf_op jit(solution)/shard_map/all_gather | solution.py:32
  10.3 152.8 %all-gather.6.cloned.1.call-start = ((), (), s32[]{:S(2)}) async-start(), calls=%async_computation.2 | async-start | bytes 8650752 | tf_op jit(solution)/shard_map/all_gather | solution.py:37
  25.3 214.7 %all-gather.8.cloned.1.call-start = ((), (), s32[]{:S(2)}) async-start(), calls=%async_computation.3 | async-start | bytes 4718592 | tf_op jit(solution)/shard_map/all_gather | solution.py:33
  26.1 1.9 copy-start.4
  28.0 2.0 copy-start.1
  30.0 1.8 copy-start.5
  31.8 131.2 %copy-start.3 = (f32[1024,512]{0,1:T(8,128)S(1)}, f32[1024,512]{0,1:T(8,128)}, u32[]{:S(2)}) copy-start(f32[1024,512]{0,1:T(8,128)} %copy.30) | copy-start | bytes 6291460
  163.1 76.9 %copy-start.6 = (bf16[1024,512]{0,1:T(8,128)(2,1)S(1)}, bf16[1024,512]{0,1:T(8,128)(2,1)}, u32[]{:S(2)}) copy-start(bf16[1024,512]{0,1:T(8,128)(2,1)} %copy.32) | copy-start | bytes 3145732
  173.8 66.2 %copy-start.2 = (f32[1024,512]{0,1:T(8,128)S(1)}, f32[1024,512]{0,1:T(8,128)}, u32[]{:S(2)}) copy-start(f32[1024,512]{0,1:T(8,128)} %copy.33) | copy-start | bytes 6291460
Sparse Core Ops, SparseCore 0:
  11.2 79.1 all-gather.3
  92.3 70.7 all-gather.5
  165.7 74.2 all-gather.7
where the time goes:
time: 260 us; the launch traced here: 259 us
  waiting for transfers between devices  194 us (75%)
  matrix products  21.3 us (8%)
  blocking collectives  15 us (6%)
  between operations  13.8 us (5%)
  local copies, waits for them, and re-layouts  11.8 us (5%)
  other arithmetic  3.02 us (1%)
    all_gather x1, waiting for transfers between devices, body(): lax.all_gather(columns, 'tp', axis=0, tiled=True)  72.6 us
    all_gather x1, waiting for transfers between devices, body(): lax.all_gather(up_delta, 'dp', axis=0, tiled=True)  63.8 us
    all_gather x1, waiting for transfers between devices, body(): lax.all_gather(gate_delta, 'dp', axis=0, tiled=True)  57.3 us
    dot_general x2, matrix products, accumulate(): lax.dot_general(piece, deltas, (((0,), (0,)), ((), ())), preferred_elemen...  21.3 us
    all_to_all x1, blocking collectives, body(): lax.all_to_all(forget_inputs, 'dp', split_axis=1, concat_axis=0, tiled=True)  15 us
    unnamed x22, local copies, waits for them, and re-layouts  11.8 us
  transfers between devices with their start and end apart: 3, of which 3 were waited for; matrix products, arithmetic and copies ran while one was open for 8% of the time, Pallas kernels for 0%

commit v1 on v0

--- a/solution.py
+++ b/solution.py
@@ -29,7 +29,9 @@
     gate_delta = (grad_val * up_val * sig * (1.0 + gate_val * (1.0 - sig))).astype(jnp.bfloat16)
     up_delta = (grad_val * gate_val * sig).astype(jnp.bfloat16)
     gate_all, up_all = (
-        lax.all_gather(gate_delta, "dp", axis=0, tiled=True),
+        jnp.concatenate(
+            lax.all_to_all(jnp.stack([gate_delta] * lax.axis_size("dp")), "dp", 0, 0), axis=0
+        ),
         lax.all_gather(up_delta, "dp", axis=0, tiled=True),
     )
     columns = lax.all_to_all(forget_inputs, "dp", split_axis=1, concat_axis=0, tiled=True)

time: 260 us -> 218 us (0.84)
  waiting for transfers between devices: 194 us -> 145 us
  starting transfers between devices: 0.12 us -> 4.79 us
  local copies, waits for them, and re-layouts: 11.8 us -> 15.1 us
    all_to_all x0 -> x1, waiting for transfers between devices: none -> 81.7 us  [body(): lax.all_to_all(jnp.stack([gate_delta] * lax.axis_size('dp')), 'dp', 0, 0)]
    all_gather x1, waiting for transfers between devices: 72.6 us -> 0.49 us  [body(): lax.all_gather(columns, 'tp', axis=0, tiled=True)]
    all_gather x1 -> x0, waiting for transfers between devices: 57.3 us -> none  [body(): lax.all_gather(gate_delta, 'dp', axis=0, tiled=True)]
    all_to_all x0 -> x1, starting transfers between devices: none -> 4.72 us  [body(): lax.all_to_all(jnp.stack([gate_delta] * lax.axis_size('dp')), 'dp', 0, 0)]
    unnamed x22 -> x20, local copies, waits for them, and re-layouts: 11.8 us -> 11.9 us
  transfers between devices with their start and end apart: 3 -> 3, of which waited for: 3 -> 3; matrix products, arithmetic and copies ran while one was open for 8% -> 11% of each run, Pallas kernels for 0% -> 0%
where the time goes in v1:
time: 218 us
  waiting for transfers between devices  145 us (67%)
  matrix products  21.3 us (10%)
  local copies, waits for them, and re-layouts  15.1 us (7%)
  blocking collectives  15 us (7%)
  between operations  14.1 us (6%)
  starting transfers between devices  4.79 us (2%)
  other arithmetic  2.7 us (1%)
    all_to_all x1, waiting for transfers between devices, body(): lax.all_to_all(jnp.stack([gate_delta] * lax.axis_size('dp')), 'dp', 0, 0)  81.7 us
    all_gather x1, waiting for transfers between devices, body(): lax.all_gather(up_delta, 'dp', axis=0, tiled=True)  62.9 us
    dot_general x2, matrix products, accumulate(): lax.dot_general(piece, deltas, (((0,), (0,)), ((), ())), preferred_elemen...  21.3 us
    all_to_all x1, blocking collectives, body(): lax.all_to_all(forget_inputs, 'dp', split_axis=1, concat_axis=0, tiled=True)  15 us
    unnamed x20, local copies, waits for them, and re-layouts  11.9 us
    all_to_all x1, starting transfers between devices, body(): lax.all_to_all(jnp.stack([gate_delta] * lax.axis_size('dp')), 'dp', 0, 0)  4.72 us
  transfers between devices with their start and end apart: 3, of which 3 were waited for; matrix products, arithmetic and copies ran while one was open for 11% of the time, Pallas kernels for 0%

profile of v1, /device:TPU:1, one launch (start us, length us, event | category | flops | bytes accessed | tf_op | source)
XLA Modules:
  0.0 218.2 jit_solution(3457463135117285330)
XLA Ops:
  7.2 0.0 all-gather.3.cloned.1.call-start
  7.2 1.0 copy.38
  8.2 15.0 %all_to_all.24 = bf16[16,8,1024]{2,0,1:T(8,128)(2,1)} all-to-all(bf16[16,8,1024]{2,0,1:T(8,128)(2,1)S(1)} %bitcast.17), channel_id=1, replica_groups=mesh['tp'=32,'dp'=8] {'dp'}, dimensions={1} | all-to-all | bytes 524288 | tf_op jit(solution)/shard_map/all_to_all | solution.py:37
  23.1 0.0 all-gather.3.cloned.1.call-update
  23.2 0.0 all-gather.5.cloned.1.call-start
  23.2 2.7 %fusion.12 = (bf16[512,512]{1,0:T(8,128)(2,1)}, bf16[512,512]{1,0:T(8,128)(2,1)S(1)}) fusion(bf16[512,512]{1,0:T(8,128)(2,1)} %param.9, bf16[512,512]{1,0:T(8,128)(2,1)} %param.11, bf16[512,512]{1,0:T(8,128)(2,1)} %param.10), kind=kLoop, calls=%fused_computation.18 | loop fusion | flops 4194304 | bytes 2621440 | tf_op jit(solution)/shard_map/convert_element_type | solution.py:30
  25.9 0.0 all-gather.5.cloned.1.call-update
  25.9 2.3 %stack.2 = bf16[8,512,512]{2,1,0:T(8,128)(2,1)} broadcast(bf16[512,512]{1,0:T(8,128)(2,1)S(1)} %get-tuple-element.11), dimensions={1,2} | broadcast | bytes 4718592 | tf_op jit(solution)/shard_map/stack | solution.py:33
  28.2 0.0 copy-start
  28.2 4.7 %all-to-all-start = ((bf16[8,512,512]{2,1,0:T(8,128)(2,1)}), bf16[8,512,512]{2,1,0:T(8,128)(2,1)}, u32[]{:S(2)}, u32[]{:S(2)}) async-start(bf16[8,512,512]{2,1,0:T(8,128)(2,1)} %stack.2), calls=%async_computation | async-start | bytes 8388608 | tf_op jit(solution)/shard_map/all_to_all | solution.py:33
  33.0 0.0 copy-done
  33.0 0.0 copy-start.4
  33.0 1.9 copy.30
  34.8 0.0 copy-done.4
  34.9 0.0 copy-start.1
  34.9 1.3 copy.29
  36.2 0.8 copy-done.1
  36.9 0.0 copy-start.5
  37.0 1.8 copy.33
  38.8 0.0 copy-done.5
  38.8 0.0 copy-start.3
  38.8 1.4 copy.32
  40.2 81.7 %all-to-all-done = bf16[8,512,512]{2,1,0:T(8,128)(2,1)} async-done(((bf16[8,512,512]{2,1,0:T(8,128)(2,1)}), bf16[8,512,512]{2,1,0:T(8,128)(2,1)}, u32[]{:S(2)}, u32[]{:S(2)}) %all-to-all-start) | async-done | bytes 4194336 | tf_op jit(solution)/shard_map/all_to_all | solution.py:33
  121.9 0.5 all-gather.3.cloned.1.call-done
  122.4 0.0 copy-done.3
  122.4 0.0 copy-start.6
  122.4 10.7 %fusion.1 = bf16[1024,512]{0,1:T(8,128)(2,1)} fusion(f32[1024,512]{0,1:T(8,128)S(1)} %copy-done.3, bf16[1024,512]{0,1:T(8,128)(2,1)} %copy.29, bf16[4096,512]{1,0:T(8,128)(2,1)} %bitcast, bf16[4096,1024]{1,0:T(8,128)(2,1)} %all-gather.3.cloned.1.call-done), kind=kOutput, calls=%fused_computation.3 | convolution fusion | flops 4299161600 | bytes 16777216 | tf_op jit(solution)/shard_map/dot_general | solution.py:11
  133.1 0.0 copy-start.2
  133.1 2.4 %copy.34 = bf16[1024,512]{1,0:T(8,128)(2,1)} copy(bf16[1024,512]{0,1:T(8,128)(2,1)} %fusion.1) | data formatting | bytes 2097152
  135.5 62.9 %all-gather.5.cloned.1.call-done = bf16[4096,512]{1,0:T(8,128)(2,1)} async-done(((bf16[512,512]{1,0:T(8,128)(2,1)}), bf16[4096,512]{1,0:T(8,128)(2,1)}) %all-gather.5.cloned.1.call-update) | async-done | bytes 4194320 | tf_op jit(solution)/shard_map/all_gather | solution.py:35
  198.5 0.0 copy-done.6
  198.5 0.0 copy-done.2
  198.5 10.6 %fusion.3 = bf16[1024,512]{0,1:T(8,128)(2,1)} fusion(f32[1024,512]{0,1:T(8,128)S(1)} %copy-done.2, bf16[1024,512]{0,1:T(8,128)(2,1)S(1)} %copy-done.6, bf16[4096,512]{1,0:T(8,128)(2,1)} %all-gather.5.cloned.1.call-done, bf16[4096,1024]{1,0:T(8,128)(2,1)} %all-gather.3.cloned.1.call-done), kind=kOutput, calls=%fused_computation.5 | convolution fusion | flops 4299161600 | bytes 16777216 | tf_op jit(solution)/shard_map/dot_general | solution.py:11
  209.0 2.3 %copy.35 = bf16[1024,512]{1,0:T(8,128)(2,1)} copy(bf16[1024,512]{0,1:T(8,128)(2,1)} %fusion.3) | data formatting | bytes 2097152
Async XLA Ops:
  7.2 115.2 %all-gather.3.cloned.1.call-start = ((), (), s32[]{:S(2)}) async-start(), calls=%async_computation.2 | async-start | bytes 8650752 | tf_op jit(solution)/shard_map/all_gather | solution.py:39
  23.2 175.3 %all-gather.5.cloned.1.call-start = ((), (), s32[]{:S(2)}) async-start(), calls=%async_computation.3 | async-start | bytes 4718592 | tf_op jit(solution)/shard_map/all_gather | solution.py:35
  28.2 4.7 %copy-start = (f32[1024,512]{1,0:T(8,128)S(1)}, f32[1024,512]{1,0:T(8,128)}, u32[]{:S(2)}) copy-start(f32[1024,512]{1,0:T(8,128)} %param.14) | copy-start | bytes 6291460
  28.2 93.6 %all-to-all-start = ((bf16[8,512,512]{2,1,0:T(8,128)(2,1)}), bf16[8,512,512]{2,1,0:T(8,128)(2,1)}, u32[]{:S(2)}, u32[]{:S(2)}) async-start(bf16[8,512,512]{2,1,0:T(8,128)(2,1)} %stack.2), calls=%async_computation | async-start | bytes 8388608 | tf_op jit(solution)/shard_map/all_to_all | solution.py:33
  33.0 1.9 copy-start.4
  34.9 2.1 copy-start.1
  36.9 1.8 copy-start.5
  38.8 83.6 %copy-start.3 = (f32[1024,512]{0,1:T(8,128)S(1)}, f32[1024,512]{0,1:T(8,128)}, u32[]{:S(2)}) copy-start(f32[1024,512]{0,1:T(8,128)} %copy.30) | copy-start | bytes 6291460
  122.4 76.1 %copy-start.6 = (bf16[1024,512]{0,1:T(8,128)(2,1)S(1)}, bf16[1024,512]{0,1:T(8,128)(2,1)}, u32[]{:S(2)}) copy-start(bf16[1024,512]{0,1:T(8,128)(2,1)} %copy.32) | copy-start | bytes 3145732
  133.1 65.4 %copy-start.2 = (f32[1024,512]{0,1:T(8,128)S(1)}, f32[1024,512]{0,1:T(8,128)}, u32[]{:S(2)}) copy-start(f32[1024,512]{0,1:T(8,128)} %copy.33) | copy-start | bytes 6291460
Sparse Core Ops, SparseCore 0:
  23.3 99.0 all-gather.2
  125.0 73.3 all-gather.4
